TPU v7x, 32 devices: a whole 2x2x4 slice. The times are simulated.
32 devices in a mesh: row: 4 (over x, core), col: 8 (over z, y).
Axes of the slice: x: 2, y: 2, z: 4, core: 2. Of those that a mesh axis runs over, the one named last changes fastest.
Arguments:
- design: bfloat16 [18432, 2048], P(('row', 'col')), may hold values from -0.19921875 to 0.19921875
- arc_filter: bfloat16 [2048, 2048], replicated, may hold values from -0.59765625 to 0.59765625
- arc_of_row: int32 [2048], replicated, may hold values from 0 to 255, never falling along the last dimension, each value on 1 to 512 neighbouring positions
- terr_stored: bfloat16 [18432, 128], P(('row', 'col')), may hold values from -3 to 3
- block_order: int32 [144], P('row'), may hold values from 0 to 143, as said below
- directions: float32 [18432, 256], P(('row', 'col')), may hold values from -6 to 6
Outputs:
- normals: float32 [4, 8, 576, 18432], P(None, 'col', None, 'row')
- products: float32 [18432, 256], P(('row', 'col'))
Inputs may be any that keep to these rules, and one draw needn't show every extreme that they name: `arc_of_row`: arc numbers never fall along the observations. `block_order`: each aligned group of 36 consecutive entries (the blocks of one block of 4608 unknowns) is a permutation of the positions of that same group.
All inputs are finite; a program needn't handle non-finite values.
Results may differ from a plain program's by a relative error of at most 0.00045.
Values may be sent and summed in bfloat16 or wider, within the bound.
A program may use at most 192 MiB of HBM per device.

v0:
```python
import jax
import jax.numpy as jnp
from jax import lax
from jax.sharding import PartitionSpec as P


def whiten(design, arc_filter, arc_of_row):
    positions = jnp.arange(arc_filter.shape[0], dtype=jnp.int32)
    keep_mask = (positions[:, None] > positions[None, :]) & (
        arc_of_row[:, None] == arc_of_row[None, :]
    )
    lower_part = jnp.where(keep_mask, arc_filter, jnp.zeros_like(arc_filter))
    mixed_part = lax.dot_general(
        design, lower_part, (((1,), (1,)), ((), ())), preferred_element_type=jnp.float32
    )
    return (design.astype(jnp.float32) + mixed_part).astype(jnp.bfloat16)


def body(design, arc_filter, arc_of_row, terr_stored, block_order, directions):
    whitened = whiten(design, arc_filter, arc_of_row)
    own_width = whitened.shape[0]
    rows_block, terr_rows = (
        lax.all_gather(whitened, "col", axis=0, tiled=True),
        lax.all_gather(terr_stored, "col", axis=0, tiled=True),
    )
    cols_block = lax.all_gather(whitened, "row", axis=0, tiled=True)
    normal_tile = lax.dot_general(
        cols_block, rows_block, (((1,), (1,)), ((), ())), preferred_element_type=jnp.float32
    )
    block_size = terr_rows.shape[1]
    span_rows = terr_rows.shape[0]
    group_count = span_rows // block_size
    row_index = lax.axis_index("row")
    col_index = lax.axis_index("col")
    local_order = block_order - row_index * group_count
    selector = (local_order[None, :] == jnp.arange(group_count, dtype=jnp.int32)[:, None]).astype(
        jnp.float32
    )
    stored = terr_rows.astype(jnp.float32).reshape(group_count, block_size, block_size)
    symmetric = jnp.triu(stored) + jnp.swapaxes(jnp.triu(stored, 1), 1, 2)
    ordered = jnp.einsum(
        "qt,tab->qab", selector, symmetric, precision=lax.Precision.HIGHEST
    ).reshape(span_rows, block_size)
    own_rows = lax.dynamic_slice_in_dim(ordered, col_index * own_width, own_width, 0)
    positions = col_index * own_width + jnp.arange(own_width, dtype=jnp.int32)
    onehot = (
        (positions // block_size)[:, None] == jnp.arange(group_count, dtype=jnp.int32)[None, :]
    ).astype(jnp.float32)
    terr_added = (onehot[:, :, None] * own_rows[:, None, :]).reshape(own_width, span_rows)
    current = lax.dynamic_slice_in_dim(normal_tile, row_index * own_width, own_width, 0)
    normal_tile = lax.dynamic_update_slice_in_dim(
        normal_tile, current + terr_added, row_index * own_width, 0
    )
    tile_rows = normal_tile.shape[0]
    partial_sum = jnp.dot(
        normal_tile,
        lax.all_gather(directions, "col", axis=0, tiled=True),
        precision=lax.Precision.HIGHEST,
        preferred_element_type=jnp.float32,
    )
    products = lax.psum_scatter(partial_sum, "row", scatter_dimension=0, tiled=True)
    normals = normal_tile.reshape(tile_rows // own_width, 1, own_width, span_rows)
    return (normals, products)


def solution(mesh):
    return jax.shard_map(
        body,
        mesh=mesh,
        in_specs=(
            P(("row", "col"), None),
            P(),
            P(),
            P(("row", "col"), None),
            P("row"),
            P(("row", "col"), None),
        ),
        out_specs=(P(None, "col", None, "row"), P(("row", "col"), None)),
        check_vma=False,
    )
```

profile of v0, /device:TPU:0, one launch (start us, length us, event | category | flops | bytes accessed | tf_op | source)
XLA Modules:
  0.0 640.6 jit_solution(7251335784853604112)
XLA Ops:
  7.2 0.0 all-gather.9.cloned.1.call-start
  7.2 0.7 all-gather.9.cloned.1.call-update
  7.9 0.0 all-gather.5.cloned.1.call-start
  7.9 11.9 %fusion.7 = bf16[576,2048]{1,0:T(8,128)(2,1)} fusion(bf16[576,2048]{1,0:T(8,128)(2,1)} %param.6, bf16[2048,2048]{1,0:T(8,128)(2,1)} %param.7, s32[2048]{0:T(1024)} %param.8), kind=kOutput, calls=%fused_computation.10 | convolution fusion | flops 4852154368 | bytes 13115392 | tf_op jit(solution)/shard_map/dot_general | solution.py:13
  19.8 0.0 copy-start.1
  19.8 0.0 all-gather.5.cloned.1.call-update
  19.8 0.0 all-gather.7.cloned.1.call-start
  19.9 0.7 all-gather.7.cloned.1.call-update
  20.6 0.0 all-gather.11.cloned.1.call-start
  20.6 0.5 all-gather.11.cloned.1.call-update
  21.1 0.0 reduce-scatter.2.cloned.1.call-start
  21.3 0.1 fusion.15
  21.4 0.0 copy-done.1
  21.4 32.6 %all-gather.9.cloned.1.call-done = bf16[4608,128]{1,0:T(8,128)(2,1)} async-done(((bf16[576,128]{1,0:T(8,128)(2,1)}), bf16[4608,128]{1,0:T(8,128)(2,1)}) %all-gather.9.cloned.1.call-update) | async-done | bytes 1179664 | tf_op jit(solution)/shard_map/all_gather | solution.py:24
  54.0 1.9 copy.12
  56.0 1.8 broadcast_select_fusion
  57.8 3.4 copy.14
  61.2 3.8 fusion.11
  65.0 0.5 copy.15
  65.5 7.0 %broadcast_multiply_fusion = f32[576,36,128]{2,1,0:T(8,128)} fusion(f32[576,128]{1,0:T(8,128)S(1)} %constant_dynamic-slice_fusion, f32[576,36]{1,0:T(8,128)S(1)} %fusion.15), kind=kLoop, calls=%fused_computation.8 | loop fusion | flops 2654208 | bytes 10994688 | tf_op jit(solution)/shard_map/mul | solution.py:49
  72.5 46.0 %all-gather.5.cloned.1.call-done = bf16[2304,2048]{1,0:T(8,128)(2,1)} async-done(((bf16[576,2048]{1,0:T(8,128)(2,1)}), bf16[2304,2048]{1,0:T(8,128)(2,1)}) %all-gather.5.cloned.1.call-update) | async-done | bytes 9437200 | tf_op jit(solution)/shard_map/all_gather | solution.py:26
  118.5 364.0 %all-gather.7.cloned.1.call-done = bf16[4608,2048]{1,0:T(8,128)(2,1)} async-done(((bf16[576,2048]{1,0:T(8,128)(2,1)}), bf16[4608,2048]{1,0:T(8,128)(2,1)}) %all-gather.7.cloned.1.call-update) | async-done | bytes 18874384 | tf_op jit(solution)/shard_map/all_gather | solution.py:23
  482.5 0.0 copy-start
  482.5 53.3 %fusion.24 = f32[2304,4608]{1,0:T(8,128)} fusion(bf16[2304,2048]{1,0:T(8,128)(2,1)} %all-gather.5.cloned.1.call-done, bf16[4608,2048]{1,0:T(8,128)(2,1)} %all-gather.7.cloned.1.call-done), kind=kOutput, calls=%fused_computation.39 | convolution fusion | flops 43486543872 | bytes 70778880 | tf_op jit(solution)/shard_map/dot_general | solution.py:27
  535.8 0.0 copy-done
  535.8 10.3 %fusion.2 = f32[2304,4608]{1,0:T(8,128)} fusion(f32[2304,4608]{1,0:T(8,128)} %fusion.24, s32[]{:T(128)S(6)} %select_n.29, f32[72,8,36,128]{3,2,1,0:T(8,128)S(1)} %bitcast.27), kind=kLoop, calls=%fused_computation.4 | loop fusion | flops 2654208 | bytes 31850500 | tf_op jit(solution)/shard_map/dynamic_update_slice | solution.py:51
  546.1 17.8 %all-gather.11.cloned.1.call-done = f32[4608,256]{1,0:T(8,128)} async-done(((f32[576,256]{1,0:T(8,128)}), f32[4608,256]{1,0:T(8,128)}) %all-gather.11.cloned.1.call-update) | async-done | bytes 4718608 | tf_op jit(solution)/shard_map/all_gather | solution.py:57
  563.9 38.9 %fusion.25 = f32[2304,256]{1,0:T(8,128)} fusion(f32[2304,4608]{1,0:T(8,128)} %fusion.2, f32[4608,256]{1,0:T(8,128)} %all-gather.11.cloned.1.call-done), kind=kOutput, calls=%fused_computation.40 | convolution fusion | flops 32614907904 | bytes 49545216 | tf_op jit(solution)/shard_map/dot_general | solution.py:55
  602.7 0.0 reduce-scatter.2.cloned.1.call-update
  602.8 31.3 %reduce-scatter.2.cloned.1.call-done = f32[576,256]{1,0:T(8,128)} async-done(((f32[2304,256]{1,0:T(8,128)}), f32[576,256]{1,0:T(8,128)}) %reduce-scatter.2.cloned.1.call-update) | async-done | bytes 589840 | tf_op jit(solution)/shard_map/reduce_scatter | solution.py:61
  (6 shorter events, 0.1 us)
Async XLA Ops:
  7.2 46.9 %all-gather.9.cloned.1.call-start = ((), (), s32[]{:S(2)}) async-start(), calls=%async_computation.3 | async-start | bytes 1327104 | tf_op jit(solution)/shard_map/all_gather | solution.py:24
  7.9 110.6 %all-gather.5.cloned.1.call-start = ((), (), s32[]{:S(2)}) async-start(), calls=%async_computation.1 | async-start | bytes 11796480 | tf_op jit(solution)/shard_map/all_gather | solution.py:26
  19.8 1.6 copy-start.1
  19.8 462.7 %all-gather.7.cloned.1.call-start = ((), (), s32[]{:S(2)}) async-start(), calls=%async_computation.2 | async-start | bytes 21233664 | tf_op jit(solution)/shard_map/all_gather | solution.py:23
  20.6 543.3 %all-gather.11.cloned.1.call-start = ((), (), s32[]{:S(2)}) async-start(), calls=%async_computation.4 | async-start | bytes 5308416 | tf_op jit(solution)/shard_map/all_gather | solution.py:57
  21.1 613.0 %reduce-scatter.2.cloned.1.call-start = ((), (), s32[]{:S(2)}) async-start(), calls=%async_computation.5 | async-start | bytes 2949120 | tf_op jit(solution)/shard_map/reduce_scatter | solution.py:61
  482.5 53.3 %copy-start = (f32[576,36,128]{2,1,0:T(8,128)S(1)}, f32[576,36,128]{2,1,0:T(8,128)}, u32[]{:S(2)}) copy-start(f32[576,36,128]{2,1,0:T(8,128)} %broadcast_multiply_fusion) | copy-start | bytes 31850500
Sparse Core Ops, SparseCore 0:
  10.2 43.8 all-gather.8
  55.6 62.8 all-gather.4
  120.1 362.3 all-gather.6
  484.5 79.2 all-gather.10
  602.9 31.1 reduce-scatter.1
where the time goes:
time: 641 us
  waiting for transfers between devices  494 us (77%)
  matrix products  108 us (17%)
  other arithmetic  19.3 us (3%)
  between operations  13.9 us (2%)
    all_gather x1, waiting for transfers between devices, body(): lax.all_gather(whitened, 'col', axis=0, tiled=True)  364 us
    dot_general x1, matrix products, body(): lax.dot_general(cols_block, rows_block, (((1,), (1,)), ((), ())), preferr...  53.3 us
    all_gather x1, waiting for transfers between devices, body(): cols_block = lax.all_gather(whitened, 'row', axis=0, tiled=True)  46 us
    dot_general x1, matrix products, body(): jnp.dot(normal_tile, lax.all_gather(directions, 'col', axis=0, tiled=True...  38.9 us
    all_gather x1, waiting for transfers between devices, body(): lax.all_gather(terr_stored, 'col', axis=0, tiled=True)  32.6 us
    reduce_scatter x1, waiting for transfers between devices, body(): lax.psum_scatter(partial_sum, 'row', scatter_dimension=0, tiled=True)  31.3 us
    all_gather x1, waiting for transfers between devices, body(): lax.all_gather(directions, 'col', axis=0, tiled=True)  17.8 us
  transfers between devices with their start and end apart: 5, of which 5 were waited for; matrix products, arithmetic and copies ran while one was open for 15% of the time, Pallas kernels for 0%

commit v1 on v0

--- a/solution.py
+++ b/solution.py
@@ -20,7 +20,9 @@
     whitened = whiten(design, arc_filter, arc_of_row)
     own_width = whitened.shape[0]
     rows_block, terr_rows = (
-        lax.all_gather(whitened, "col", axis=0, tiled=True),
+        jnp.concatenate(
+            lax.all_to_all(jnp.stack([whitened] * lax.axis_size("col")), "col", 0, 0), axis=0
+        ),
         lax.all_gather(terr_stored, "col", axis=0, tiled=True),
     )
     cols_block = lax.all_gather(whitened, "row", axis=0, tiled=True)

time: 641 us -> 677 us (1.056)
  waiting for transfers between devices: 494 us -> 516 us
  local copies, waits for them, and re-layouts: 5.85 us -> 13.3 us
  starting transfers between devices: 0.19 us -> 7.59 us
    all_gather x1, waiting for transfers between devices: 32.6 us -> 420 us  [body(): lax.all_gather(terr_stored, 'col', axis=0, tiled=True)]
    all_gather x1 -> x0, waiting for transfers between devices: 364 us -> none  [body(): lax.all_gather(whitened, 'col', axis=0, tiled=True)]
    all_to_all x0 -> x1, starting transfers between devices: none -> 7.44 us  [body(): lax.all_to_all(jnp.stack([whitened] * lax.axis_size('col')), 'col', 0, 0)]
    another operation x0 -> x1, local copies, waits for them, and re-layouts: none -> 7.19 us  [body(): jnp.stack([whitened] * lax.axis_size('col'))]
  transfers between devices with their start and end apart: 5 -> 5, of which waited for: 5 -> 4; matrix products, arithmetic and copies ran while one was open for 15% -> 12% of each run, Pallas kernels for 0% -> 0%
where the time goes in v1:
time: 677 us
  waiting for transfers between devices  516 us (76%)
  matrix products  107 us (16%)
  other arithmetic  19.3 us (3%)
  between operations  13.9 us (2%)
  local copies, waits for them, and re-layouts  13.3 us (2%)
  starting transfers between devices  7.59 us (1%)
    all_gather x1, waiting for transfers between devices, body(): lax.all_gather(terr_stored, 'col', axis=0, tiled=True)  420 us
    dot_general x1, matrix products, body(): lax.dot_general(cols_block, rows_block, (((1,), (1,)), ((), ())), preferr...  53.3 us
    all_gather x1, waiting for transfers between devices, body(): cols_block = lax.all_gather(whitened, 'row', axis=0, tiled=True)  44.3 us
    dot_general x1, matrix products, body(): jnp.dot(normal_tile, lax.all_gather(directions, 'col', axis=0, tiled=True...  38.9 us
    reduce_scatter x1, waiting for transfers between devices, body(): lax.psum_scatter(partial_sum, 'row', scatter_dimension=0, tiled=True)  31.3 us
    all_gather x1, waiting for transfers between devices, body(): lax.all_gather(directions, 'col', axis=0, tiled=True)  18 us
  transfers between devices with their start and end apart: 5, of which 4 were waited for; matrix products, arithmetic and copies ran while one was open for 12% of the time, Pallas kernels for 0%

profile of v1, /device:TPU:0, one launch (start us, length us, event | category | flops | bytes accessed | tf_op | source)
XLA Modules:
  0.0 676.8 jit_solution(2122635762939635738)
XLA Ops:
  7.2 10.8 %fusion.7 = bf16[576,2048]{1,0:T(8,128)(2,1)S(1)} fusion(bf16[576,2048]{1,0:T(8,128)(2,1)} %param.6, bf16[2048,2048]{1,0:T(8,128)(2,1)} %param.7, s32[2048]{0:T(1024)} %param.8), kind=kOutput, calls=%fused_computation.10 | convolution fusion | flops 4852154368 | bytes 13115392 | tf_op jit(solution)/shard_map/dot_general | solution.py:13
  18.0 0.0 copy-start.1
  18.0 7.2 %stack.2 = bf16[8,576,2048]{2,1,0:T(8,128)(2,1)} broadcast(bf16[576,2048]{1,0:T(8,128)(2,1)S(1)} %fusion.7), dimensions={1,2} | broadcast | bytes 21233664 | tf_op jit(solution)/shard_map/stack | solution.py:24
  25.2 0.0 copy-done.1
  25.2 0.0 copy-start.2
  25.2 7.4 %all-to-all-start = ((bf16[8,576,2048]{2,1,0:T(8,128)(2,1)}), bf16[8,576,2048]{2,1,0:T(8,128)(2,1)}, u32[]{:S(2)}, u32[]{:S(2)}) async-start(bf16[8,576,2048]{2,1,0:T(8,128)(2,1)} %stack.2), calls=%async_computation | async-start | bytes 37748736 | tf_op jit(solution)/shard_map/all_to_all | solution.py:24
  32.6 0.0 all-gather.6.cloned.1.call-start
  32.6 0.7 all-gather.6.cloned.1.call-update
  33.3 0.0 all-gather.4.cloned.1.call-start
  33.4 0.7 all-gather.4.cloned.1.call-update
  34.1 0.0 all-gather.8.cloned.1.call-start
  34.1 0.7 all-gather.8.cloned.1.call-update
  34.8 0.0 reduce-scatter.2.cloned.1.call-start
  34.9 0.0 copy-done.2
  35.0 0.1 fusion.15
  35.1 420.3 %all-gather.6.cloned.1.call-done = bf16[4608,128]{1,0:T(8,128)(2,1)} async-done(((bf16[576,128]{1,0:T(8,128)(2,1)}), bf16[4608,128]{1,0:T(8,128)(2,1)}) %all-gather.6.cloned.1.call-update) | async-done | bytes 1179664 | tf_op jit(solution)/shard_map/all_gather | solution.py:26
  455.5 1.9 copy.12
  457.4 1.8 broadcast_select_fusion
  459.2 3.7 copy.14
  462.9 3.8 fusion.11
  466.7 0.5 copy.15
  467.2 7.0 %broadcast_multiply_fusion = f32[576,36,128]{2,1,0:T(8,128)} fusion(f32[576,128]{1,0:T(8,128)S(1)} %constant_dynamic-slice_fusion, f32[576,36]{1,0:T(8,128)S(1)} %fusion.15), kind=kLoop, calls=%fused_computation.8 | loop fusion | flops 2654208 | bytes 10994688 | tf_op jit(solution)/shard_map/mul | solution.py:51
  474.2 44.3 %all-gather.4.cloned.1.call-done = bf16[2304,2048]{1,0:T(8,128)(2,1)} async-done(((bf16[576,2048]{1,0:T(8,128)(2,1)}), bf16[2304,2048]{1,0:T(8,128)(2,1)}) %all-gather.4.cloned.1.call-update) | async-done | bytes 9437200 | tf_op jit(solution)/shard_map/all_gather | solution.py:28
  518.5 0.0 all-to-all-done
  518.5 0.0 copy-start
  518.5 53.3 %fusion.24 = f32[2304,4608]{1,0:T(8,128)} fusion(bf16[2304,2048]{1,0:T(8,128)(2,1)} %all-gather.4.cloned.1.call-done, bf16[4608,2048]{1,0:T(8,128)(2,1)} %bitcast.1), kind=kOutput, calls=%fused_computation.39 | convolution fusion | flops 43486543872 | bytes 70778880 | tf_op jit(solution)/shard_map/dot_general | solution.py:29
  571.8 0.0 copy-done
  571.8 10.3 %fusion.2 = f32[2304,4608]{1,0:T(8,128)} fusion(f32[2304,4608]{1,0:T(8,128)} %fusion.24, s32[]{:T(128)S(6)} %select_n.29, f32[72,8,36,128]{3,2,1,0:T(8,128)S(1)} %bitcast.28), kind=kLoop, calls=%fused_computation.4 | loop fusion | flops 2654208 | bytes 31850500 | tf_op jit(solution)/shard_map/dynamic_update_slice | solution.py:53
  582.0 18.0 %all-gather.8.cloned.1.call-done = f32[4608,256]{1,0:T(8,128)} async-done(((f32[576,256]{1,0:T(8,128)}), f32[4608,256]{1,0:T(8,128)}) %all-gather.8.cloned.1.call-update) | async-done | bytes 4718608 | tf_op jit(solution)/shard_map/all_gather | solution.py:59
  600.0 38.9 %fusion.25 = f32[2304,256]{1,0:T(8,128)} fusion(f32[2304,4608]{1,0:T(8,128)} %fusion.2, f32[4608,256]{1,0:T(8,128)} %all-gather.8.cloned.1.call-done), kind=kOutput, calls=%fused_computation.40 | convolution fusion | flops 32614907904 | bytes 49545216 | tf_op jit(solution)/shard_map/dot_general | solution.py:57
  638.9 0.0 reduce-scatter.2.cloned.1.call-update
  638.9 31.3 %reduce-scatter.2.cloned.1.call-done = f32[576,256]{1,0:T(8,128)} async-done(((f32[2304,256]{1,0:T(8,128)}), f32[576,256]{1,0:T(8,128)}) %reduce-scatter.2.cloned.1.call-update) | async-done | bytes 589840 | tf_op jit(solution)/shard_map/reduce_scatter | solution.py:63
  (6 shorter events, 0.1 us)
Async XLA Ops:
  18.0 7.2 %copy-start.1 = (bf16[576,2048]{1,0:T(8,128)(2,1)}, bf16[576,2048]{1,0:T(8,128)(2,1)S(1)}, u32[]{:S(2)}) copy-start(bf16[576,2048]{1,0:T(8,128)(2,1)S(1)} %fusion.7) | copy-start | bytes 7077892
  25.2 9.8 %copy-start.2 = (s32[36]{0:T(128)S(1)}, s32[36]{0:T(128)}, u32[]{:S(2)}) copy-start(s32[36]{0:T(128)} %param.10) | copy-start | bytes 436
  25.2 493.3 %all-to-all-start = ((bf16[8,576,2048]{2,1,0:T(8,128)(2,1)}), bf16[8,576,2048]{2,1,0:T(8,128)(2,1)}, u32[]{:S(2)}, u32[]{:S(2)}) async-start(bf16[8,576,2048]{2,1,0:T(8,128)(2,1)} %stack.2), calls=%async_computation | async-start | bytes 37748736 | tf_op jit(solution)/shard_map/all_to_all | solution.py:24
  32.6 422.9 %all-gather.6.cloned.1.call-start = ((), (), s32[]{:S(2)}) async-start(), calls=%async_computation.3 | async-start | bytes 1327104 | tf_op jit(solution)/shard_map/all_gather | solution.py:26
  33.3 485.1 %all-gather.4.cloned.1.call-start = ((), (), s32[]{:S(2)}) async-start(), calls=%async_computation.2 | async-start | bytes 11796480 | tf_op jit(solution)/shard_map/all_gather | solution.py:28
  34.1 565.9 %all-gather.8.cloned.1.call-start = ((), (), s32[]{:S(2)}) async-start(), calls=%async_computation.4 | async-start | bytes 5308416 | tf_op jit(solution)/shard_map/all_gather | solution.py:59
  34.8 635.4 %reduce-scatter.2.cloned.1.call-start = ((), (), s32[]{:S(2)}) async-start(), calls=%async_computation.5 | async-start | bytes 2949120 | tf_op jit(solution)/shard_map/reduce_scatter | solution.py:63
  518.5 53.3 %copy-start = (f32[576,36,128]{2,1,0:T(8,128)S(1)}, f32[576,36,128]{2,1,0:T(8,128)}, u32[]{:S(2)}) copy-start(f32[576,36,128]{2,1,0:T(8,128)} %broadcast_multiply_fusion) | copy-start | bytes 31850500
Sparse Core Ops, SparseCore 0:
  35.6 419.8 all-gather.5
  457.0 61.4 all-gather.3
  520.7 79.3 all-gather.7
  639.1 31.1 reduce-scatter.1
